TPU v7x, 32 devices: a whole 2x2x4 slice. The times are simulated.
32 devices in a mesh: tm: 8 (over z, y), space: 4 (over x, core).
Axes of the slice: x: 2, y: 2, z: 4, core: 2. Of those that a mesh axis runs over, the one named last changes fastest.
Arguments:
- initial_guess: float32 [8, 1024, 1024], P('tm', 'space'), may hold values from -6 to 6
- start_field: float32 [1024, 1024], P('space'), may hold values from -6 to 6
- source_field: float32 [1024, 1024], P('space'), may hold values from -0.3 to 0.3
Outputs:
- final_states: float32 [8, 1024, 1024], P('tm', 'space')
All inputs are finite; a program needn't handle non-finite values.
Results may differ from a plain program's by a relative error of at most 0.00013.
Values sent between devices are 32-bit elements; how exact they have to be, the bound alone decides.
A program may use at most 64 MiB of HBM per device.

v0:
```python
import jax
import jax.numpy as jnp
from jax import lax
from jax.sharding import PartitionSpec as P

M = 16
decay_rate = 0.0005
spread_rate = 0.01


def shifted(value, axis, steps):
    count = lax.axis_size(axis)
    first, last = (max(0, -steps), min(count, count - steps))
    return lax.ppermute(value, axis, [(source, source + steps) for source in range(first, last)])


def cas_matrix(length):
    indices = jnp.arange(length, dtype=jnp.int32)
    product = indices[:, None] * indices[None, :] % length
    angles = 2.0 * jnp.pi / length * product.astype(jnp.float32)
    return jnp.cos(angles) + jnp.sin(angles)


def local_symbols(length, column_width):
    offset = lax.axis_index("space") * column_width
    row_modes = jnp.arange(length, dtype=jnp.int32).astype(jnp.float32)
    column_modes = (offset + jnp.arange(column_width, dtype=jnp.int32)).astype(jnp.float32)
    row_sines = jnp.sin(jnp.pi * row_modes / length) ** 2
    column_sines = jnp.sin(jnp.pi * column_modes / length) ** 2
    stiffness = 4.0 * (row_sines[:, None] + column_sines[None, :])
    fine_factor = 1.0 / (1.0 + decay_rate + spread_rate * stiffness)
    coarse_factor = 1.0 / (1.0 + M * decay_rate + M * spread_rate * stiffness)
    fine_power = jnp.ones_like(fine_factor)
    forcing_symbol = jnp.zeros_like(fine_factor)
    for substep in range(M):
        fine_power = fine_power * fine_factor
        forcing_symbol = forcing_symbol + fine_power
    return (fine_power, forcing_symbol, coarse_factor)


def forward(fields, kernel):
    along_rows = jnp.einsum("brj,jk->brk", fields, kernel, precision=lax.Precision.HIGHEST)
    columns = lax.all_to_all(along_rows, "space", split_axis=2, concat_axis=1, tiled=True)
    return jnp.einsum("ij,bjk->bik", kernel, columns, precision=lax.Precision.HIGHEST)


def inverse(spectra, kernel):
    length = kernel.shape[0]
    along_columns = jnp.einsum("ij,bjk->bik", kernel, spectra, precision=lax.Precision.HIGHEST)
    row_layout = lax.all_to_all(along_columns, "space", split_axis=1, concat_axis=2, tiled=True)
    restored = jnp.einsum("brj,jk->brk", row_layout, kernel, precision=lax.Precision.HIGHEST)
    return restored / float(length * length)


def previous(states, start_state, at_start):
    incoming = shifted(states[-1], "tm", 1)
    first_state = jnp.where(at_start, start_state, incoming)
    return jnp.concatenate([first_state[None], states[:-1]], axis=0)


def coarse_chain(residual_hat, coarse_factor):
    blocks = residual_hat.shape[0]
    running = jnp.zeros_like(residual_hat[0])
    position = 0
    running = coarse_factor * running + residual_hat[position]
    partial_value = [running]
    block_factor = coarse_factor**blocks
    relay_turns = lax.axis_size("tm") - 1

    def relay_turn(turn_index, carried):
        outgoing = block_factor * carried + running
        return shifted(outgoing, "tm", 1)

    entering = lax.fori_loop(0, relay_turns, relay_turn, jnp.zeros_like(running))
    lifting = jnp.ones_like(coarse_factor)
    position = 0
    lifting = lifting * coarse_factor
    errors = [partial_value[position] + lifting * entering]
    return jnp.stack(errors, axis=0)


def body(initial_guess, start_field, source_field):
    length = start_field.shape[1]
    column_width = length // lax.axis_size("space")
    kernel = cas_matrix(length)
    fine_power, forcing_symbol, coarse_factor = local_symbols(length, column_width)
    at_start = lax.axis_index("tm") == 0
    blocks = initial_guess.shape[0]
    stacked = jnp.concatenate([initial_guess, start_field[None], source_field[None]], axis=0)
    spectra = forward(stacked, kernel)
    states = spectra[:blocks]
    start_state = spectra[blocks]
    forcing = forcing_symbol * spectra[blocks + 1]
    relaxed = fine_power * previous(states, start_state, at_start) + forcing
    residual = fine_power * previous(relaxed, start_state, at_start) + forcing - relaxed
    states = relaxed + coarse_chain(residual, coarse_factor)
    return inverse(states, kernel)


def solution(mesh):
    return jax.shard_map(
        body,
        mesh=mesh,
        in_specs=(P("tm", "space", None), P("space", None), P("space", None)),
        out_specs=P("tm", "space", None),
        check_vma=False,
    )
```

profile of v0, /device:TPU:16, one launch (start us, length us, event | category | flops | bytes accessed | tf_op | source)
XLA Modules:
  0.0 402.9 jit_solution(6113995466226512795)
XLA Ops:
  0.0 2.1 fusion.99
  2.1 28.3 %fusion.8 = f32[3,256,1024]{2,1,0:T(8,128)S(1)} fusion(f32[3,256,1024]{2,1,0:T(8,128)S(1)} %fusion.99), kind=kOutput, calls=%fused_computation.11 | convolution fusion | flops 9679405056 | bytes 6291456 | tf_op jit(solution)/shard_map/brj,jk->brk/dot_general | solution.py:42
  30.4 3.3 copy.19
  33.6 5.3 %all-to-all-start = ((f32[3,256,1024]{1,0,2:T(4,128)}), f32[3,256,1024]{1,0,2:T(4,128)}, u32[]{:S(2)}, u32[]{:S(2)}) async-start(f32[3,256,1024]{1,0,2:T(4,128)} %copy.19), calls=%async_computation | async-start | bytes 8388608 | tf_op jit(solution)/shard_map/all_to_all | solution.py:43
  38.9 17.5 %fusion.101 = f32[1024,1024,1]{1,0,2:T(8,128)} fusion(), kind=kLoop, calls=%fused_computation.10.clone.clone.clone.1 | loop fusion | flops 15728640 | bytes 4194304 | tf_op jit(solution)/shard_map/ij,bjk->bik/dot_general | solution.py:44
  56.4 30.7 %all-to-all-done = f32[3,256,1024]{1,0,2:T(4,128)} async-done(((f32[3,256,1024]{1,0,2:T(4,128)}), f32[3,256,1024]{1,0,2:T(4,128)}, u32[]{:S(2)}, u32[]{:S(2)}) %all-to-all-start) | async-done | bytes 3145760 | tf_op jit(solution)/shard_map/all_to_all | solution.py:43
  87.1 4.2 %copy.28 = f32[3,256,4,256]{1,2,3,0:T(4,128)S(1)} copy(f32[3,256,4,256]{1,0,3,2:T(4,128)} %bitcast.3) | data formatting | bytes 6291456 | tf_op jit(solution)/shard_map/all_to_all | solution.py:43
  91.3 3.1 all_to_all.27
  94.4 13.3 %fusion.20 = f32[3,1024,256]{1,2,0:T(8,128)S(1)} fusion(f32[3,1024,256]{1,2,0:T(8,128)} %all_to_all.27, f32[1024,1024,1]{1,0,2:T(8,128)} %fusion.101), kind=kOutput, calls=%fused_computation.27 | convolution fusion | flops 9663676416 | bytes 10485760 | tf_op jit(solution)/shard_map/ij,bjk->bik/dot_general | solution.py:44
  107.7 1.0 slice_bitcast_fusion.1
  108.7 3.4 collective-permute-start.1
  112.2 24.2 %collective-permute-done.1 = f32[1024,256]{0,1:T(8,128)} collective-permute-done((f32[1024,256]{0,1:T(8,128)}, f32[1024,256]{0,1:T(8,128)}, u32[]{:S(2)}, u32[]{:S(2)}) %collective-permute-start.1) | collective-permute-done | bytes 1048608 | tf_op jit(solution)/shard_map/ppermute | solution.py:14
  136.4 2.6 multiply_add_fusion.1
  139.0 0.0 copy-start
  139.0 2.5 collective-permute-start.2
  141.5 24.0 %collective-permute-done.2 = f32[1024,256]{0,1:T(8,128)S(1)} collective-permute-done((f32[1024,256]{0,1:T(8,128)S(1)}, f32[1024,256]{0,1:T(8,128)S(1)}, u32[]{:S(2)}, u32[]{:S(2)}) %collective-permute-start.2) | collective-permute-done | bytes 1048608 | tf_op jit(solution)/shard_map/ppermute | solution.py:14
  165.5 0.0 copy-done
  165.5 2.0 subtract_add_fusion
  167.5 1.6 copy.22
  169.1 0.1 broadcast.36.clone
  169.2 166.4 %while.11 = (s32[]{:T(128)}, f32[1024,256]{1,0:T(8,128)S(1)}, f32[1024,256]{1,0:T(8,128)S(1)}, f32[256]{0:T(256)S(1)}, f32[1024]{0:T(1024)S(1)}, /*index=5*/s32[]{:T(128)}) while((s32[]{:T(128)}, f32[1024,256]{1,0:T(8,128)S(1)}, f32[1024,256]{1,0:T(8,128)S(1)}, f32[256]{0:T(256)S(1)}, f32[1024]{0:T(1024)S(1)}, ...), condition=%wide.region_1.2_spmd.clone, body=%wide.region_0.1_spmd.clone.sunk | while | flops 1572866 | bytes 7345261 | solution.py:74
  169.4 0.3 fusion.104
  169.6 1.9 collective-permute-start
  171.6 23.7 %collective-permute-done = f32[1024,256]{1,0:T(8,128)S(1)} collective-permute-done((f32[1024,256]{1,0:T(8,128)S(1)}, f32[1024,256]{1,0:T(8,128)S(1)}, u32[]{:S(2)}, u32[]{:S(2)}) %collective-permute-start) | collective-permute-done | bytes 1048608 | tf_op jit(solution)/shard_map/while/body/eval_jaxpr/ppermute | solution.py:14
  195.3 0.3 fusion.104
  195.6 1.9 collective-permute-start
  197.5 22.9 %collective-permute-done = f32[1024,256]{1,0:T(8,128)S(1)} collective-permute-done((f32[1024,256]{1,0:T(8,128)S(1)}, f32[1024,256]{1,0:T(8,128)S(1)}, u32[]{:S(2)}, u32[]{:S(2)}) %collective-permute-start) | collective-permute-done | bytes 1048608 | tf_op jit(solution)/shard_map/while/body/eval_jaxpr/ppermute | solution.py:14
  220.4 0.3 fusion.104
  220.7 1.9 collective-permute-start
  222.6 22.0 %collective-permute-done = f32[1024,256]{1,0:T(8,128)S(1)} collective-permute-done((f32[1024,256]{1,0:T(8,128)S(1)}, f32[1024,256]{1,0:T(8,128)S(1)}, u32[]{:S(2)}, u32[]{:S(2)}) %collective-permute-start) | collective-permute-done | bytes 1048608 | tf_op jit(solution)/shard_map/while/body/eval_jaxpr/ppermute | solution.py:14
  244.7 0.3 fusion.104
  245.0 1.9 collective-permute-start
  246.9 21.2 %collective-permute-done = f32[1024,256]{1,0:T(8,128)S(1)} collective-permute-done((f32[1024,256]{1,0:T(8,128)S(1)}, f32[1024,256]{1,0:T(8,128)S(1)}, u32[]{:S(2)}, u32[]{:S(2)}) %collective-permute-start) | collective-permute-done | bytes 1048608 | tf_op jit(solution)/shard_map/while/body/eval_jaxpr/ppermute | solution.py:14
  268.1 0.3 fusion.104
  268.4 1.9 collective-permute-start
  270.3 21.1 %collective-permute-done = f32[1024,256]{1,0:T(8,128)S(1)} collective-permute-done((f32[1024,256]{1,0:T(8,128)S(1)}, f32[1024,256]{1,0:T(8,128)S(1)}, u32[]{:S(2)}, u32[]{:S(2)}) %collective-permute-start) | collective-permute-done | bytes 1048608 | tf_op jit(solution)/shard_map/while/body/eval_jaxpr/ppermute | solution.py:14
  291.4 0.3 fusion.104
  291.7 1.9 collective-permute-start
  293.6 21.1 %collective-permute-done = f32[1024,256]{1,0:T(8,128)S(1)} collective-permute-done((f32[1024,256]{1,0:T(8,128)S(1)}, f32[1024,256]{1,0:T(8,128)S(1)}, u32[]{:S(2)}, u32[]{:S(2)}) %collective-permute-start) | collective-permute-done | bytes 1048608 | tf_op jit(solution)/shard_map/while/body/eval_jaxpr/ppermute | solution.py:14
  314.7 0.3 fusion.104
  315.0 1.9 collective-permute-start
  316.9 18.6 %collective-permute-done = f32[1024,256]{1,0:T(8,128)S(1)} collective-permute-done((f32[1024,256]{1,0:T(8,128)S(1)}, f32[1024,256]{1,0:T(8,128)S(1)}, u32[]{:S(2)}, u32[]{:S(2)}) %collective-permute-start) | collective-permute-done | bytes 1048608 | tf_op jit(solution)/shard_map/while/body/eval_jaxpr/ppermute | solution.py:14
  335.5 0.3 copy.23
  335.9 22.8 %fusion.27 = f32[1,1024,256]{1,2,0:T(8,128)S(1)} fusion(f32[1024,256]{0,1:T(8,128)} %copy-done, f32[1024,256]{0,1:T(8,128)} %subtract_add_fusion, f32[1024,256]{0,1:T(8,128)S(1)} %copy.23, f32[256]{0:T(256)S(1)} %get-tuple-element.130, f32[1024]{0:T(1024)S(1)} %get-tuple-element.129), kind=kOutput, calls=%fused_computation.34 | convolution fusion | flops 3238789120 | bytes 4199424 | tf_op jit(solution)/shard_map/ij,bjk->bik/dot_general | solution.py:49
  358.7 0.8 copy.24
  359.5 18.6 %all_to_all.33 = f32[1,1024,256]{2,0,1:T(1,128)S(1)} all-to-all(f32[1,1024,256]{2,0,1:T(1,128)S(1)} %copy.24), channel_id=1, replica_groups=mesh['tm'=8,'space'=4] {'space'}, dimensions={1} | all-to-all | bytes 2097152 | tf_op jit(solution)/shard_map/all_to_all | solution.py:50
  378.1 0.1 copy.26
  378.2 0.3 copy.25
  378.5 24.2 %fusion.29 = f32[1,256,1024]{2,1,0:T(8,128)} fusion(f32[256,1024]{0,1:T(8,128)S(1)} %bitcast.54), kind=kOutput, calls=%fused_computation.36 | convolution fusion | flops 3237216256 | bytes 2097152 | tf_op jit(solution)/shard_map/brj,jk->brk/dot_general | solution.py:51
  (2 shorter events, 0.1 us)
Async XLA Ops:
  33.6 53.5 %all-to-all-start = ((f32[3,256,1024]{1,0,2:T(4,128)}), f32[3,256,1024]{1,0,2:T(4,128)}, u32[]{:S(2)}, u32[]{:S(2)}) async-start(f32[3,256,1024]{1,0,2:T(4,128)} %copy.19), calls=%async_computation | async-start | bytes 8388608 | tf_op jit(solution)/shard_map/all_to_all | solution.py:43
  108.7 27.7 %collective-permute-start.1 = (f32[1024,256]{0,1:T(8,128)}, f32[1024,256]{0,1:T(8,128)}, u32[]{:S(2)}, u32[]{:S(2)}) collective-permute-start(f32[1024,256]{0,1:T(8,128)} %slice_bitcast_fusion.1), channel_id=1, source_target_pairs={{0,4},{4,8},{8,12},{12,16},{16,20},{20,24},{24,28},{1,5},{5,9},{9,... | collective-permute-start | bytes 3145736 | tf_op jit(solution)/shard_map/ppermute | solution.py:14
  139.0 26.5 %copy-start = (f32[1024,256]{0,1:T(8,128)}, f32[1024,256]{0,1:T(8,128)S(1)}, u32[]{:S(2)}) copy-start(f32[1024,256]{0,1:T(8,128)S(1)} %get-tuple-element.72) | copy-start | bytes 3145732
  139.0 26.5 %collective-permute-start.2 = (f32[1024,256]{0,1:T(8,128)S(1)}, f32[1024,256]{0,1:T(8,128)S(1)}, u32[]{:S(2)}, u32[]{:S(2)}) collective-permute-start(f32[1024,256]{0,1:T(8,128)S(1)} %get-tuple-element.72), channel_id=1, source_target_pairs={{0,4},{4,8},{8,12},{12,16},{16,20},{20,24},{24,28},{1,5},{5,9},{9,... | collective-permute-start | bytes 3145736 | tf_op jit(solution)/shard_map/ppermute | solution.py:14
  169.6 25.7 %collective-permute-start = (f32[1024,256]{1,0:T(8,128)S(1)}, f32[1024,256]{1,0:T(8,128)S(1)}, u32[]{:S(2)}, u32[]{:S(2)}) collective-permute-start(f32[1024,256]{1,0:T(8,128)S(1)} %fusion.104), channel_id=1, source_target_pairs={{0,4},{4,8},{8,12},{12,16},{16,20},{20,24},{24,28},{1,5},{5,9},{9,... | collective-permute-start | bytes 3145736 | tf_op jit(solution)/shard_map/while/body/eval_jaxpr/ppermute | solution.py:14
  195.6 24.8 %collective-permute-start = (f32[1024,256]{1,0:T(8,128)S(1)}, f32[1024,256]{1,0:T(8,128)S(1)}, u32[]{:S(2)}, u32[]{:S(2)}) collective-permute-start(f32[1024,256]{1,0:T(8,128)S(1)} %fusion.104), channel_id=1, source_target_pairs={{0,4},{4,8},{8,12},{12,16},{16,20},{20,24},{24,28},{1,5},{5,9},{9,... | collective-permute-start | bytes 3145736 | tf_op jit(solution)/shard_map/while/body/eval_jaxpr/ppermute | solution.py:14
  220.7 24.0 %collective-permute-start = (f32[1024,256]{1,0:T(8,128)S(1)}, f32[1024,256]{1,0:T(8,128)S(1)}, u32[]{:S(2)}, u32[]{:S(2)}) collective-permute-start(f32[1024,256]{1,0:T(8,128)S(1)} %fusion.104), channel_id=1, source_target_pairs={{0,4},{4,8},{8,12},{12,16},{16,20},{20,24},{24,28},{1,5},{5,9},{9,... | collective-permute-start | bytes 3145736 | tf_op jit(solution)/shard_map/while/body/eval_jaxpr/ppermute | solution.py:14
  245.0 23.1 %collective-permute-start = (f32[1024,256]{1,0:T(8,128)S(1)}, f32[1024,256]{1,0:T(8,128)S(1)}, u32[]{:S(2)}, u32[]{:S(2)}) collective-permute-start(f32[1024,256]{1,0:T(8,128)S(1)} %fusion.104), channel_id=1, source_target_pairs={{0,4},{4,8},{8,12},{12,16},{16,20},{20,24},{24,28},{1,5},{5,9},{9,... | collective-permute-start | bytes 3145736 | tf_op jit(solution)/shard_map/while/body/eval_jaxpr/ppermute | solution.py:14
  268.4 23.0 %collective-permute-start = (f32[1024,256]{1,0:T(8,128)S(1)}, f32[1024,256]{1,0:T(8,128)S(1)}, u32[]{:S(2)}, u32[]{:S(2)}) collective-permute-start(f32[1024,256]{1,0:T(8,128)S(1)} %fusion.104), channel_id=1, source_target_pairs={{0,4},{4,8},{8,12},{12,16},{16,20},{20,24},{24,28},{1,5},{5,9},{9,... | collective-permute-start | bytes 3145736 | tf_op jit(solution)/shard_map/while/body/eval_jaxpr/ppermute | solution.py:14
  291.7 23.0 %collective-permute-start = (f32[1024,256]{1,0:T(8,128)S(1)}, f32[1024,256]{1,0:T(8,128)S(1)}, u32[]{:S(2)}, u32[]{:S(2)}) collective-permute-start(f32[1024,256]{1,0:T(8,128)S(1)} %fusion.104), channel_id=1, source_target_pairs={{0,4},{4,8},{8,12},{12,16},{16,20},{20,24},{24,28},{1,5},{5,9},{9,... | collective-permute-start | bytes 3145736 | tf_op jit(solution)/shard_map/while/body/eval_jaxpr/ppermute | solution.py:14
  315.0 20.5 %collective-permute-start = (f32[1024,256]{1,0:T(8,128)S(1)}, f32[1024,256]{1,0:T(8,128)S(1)}, u32[]{:S(2)}, u32[]{:S(2)}) collective-permute-start(f32[1024,256]{1,0:T(8,128)S(1)} %fusion.104), channel_id=1, source_target_pairs={{0,4},{4,8},{8,12},{12,16},{16,20},{20,24},{24,28},{1,5},{5,9},{9,... | collective-permute-start | bytes 3145736 | tf_op jit(solution)/shard_map/while/body/eval_jaxpr/ppermute | solution.py:14
where the time goes:
time: 409 us; the launch traced here: 403 us
  waiting for transfers between devices  229 us (56%)
  matrix products  88.5 us (22%)
  other arithmetic  26.2 us (6%)
  starting transfers between devices  24.7 us (6%)
  blocking collectives  18.6 us (5%)
  local copies, waits for them, and re-layouts  14.7 us (4%)
    ppermute x9, waiting for transfers between devices, shifted(): lax.ppermute(value, axis, [(source, source + steps) for source in range(f...  199 us
    all_to_all x1, waiting for transfers between devices, forward(): lax.all_to_all(along_rows, 'space', split_axis=2, concat_axis=1, tiled=True)  30.7 us
    dot_general x1, matrix products, forward(): jnp.einsum('brj,jk->brk', fields, kernel, precision=lax.Precision.HIGHEST)  28.3 us
    dot_general x1, matrix products, inverse(): jnp.einsum('brj,jk->brk', row_layout, kernel, precision=lax.Precision.HIG...  24.2 us
    dot_general x1, matrix products, inverse(): jnp.einsum('ij,bjk->bik', kernel, spectra, precision=lax.Precision.HIGHEST)  22.8 us
    ppermute x9, starting transfers between devices, shifted(): lax.ppermute(value, axis, [(source, source + steps) for source in range(f...  19.4 us
    all_to_all x1, blocking collectives, inverse(): lax.all_to_all(along_columns, 'space', split_axis=1, concat_axis=2, tiled...  18.6 us
    dot_general x1, other arithmetic, forward(): jnp.einsum('ij,bjk->bik', kernel, columns, precision=lax.Precision.HIGHEST)  17.5 us
  transfers between devices with their start and end apart: 10, of which 10 were waited for; matrix products, arithmetic and copies ran while one was open for 4% of the time, Pallas kernels for 0%

commit v1 on v0

--- a/solution.py
+++ b/solution.py
@@ -40,7 +40,10 @@
 
 def forward(fields, kernel):
     along_rows = jnp.einsum("brj,jk->brk", fields, kernel, precision=lax.Precision.HIGHEST)
-    columns = lax.all_to_all(along_rows, "space", split_axis=2, concat_axis=1, tiled=True)
+    n_dev = lax.axis_size("space")
+    parts = jnp.stack(jnp.split(along_rows, n_dev, axis=2), axis=0)
+    parts = lax.all_to_all(parts, "space", split_axis=0, concat_axis=0)
+    columns = jnp.concatenate(parts, axis=1)
     return jnp.einsum("ij,bjk->bik", kernel, columns, precision=lax.Precision.HIGHEST)
 
 

time: 409 us -> 399 us (0.976)
  waiting for transfers between devices: 229 us -> 218 us
  local copies, waits for them, and re-layouts: 14.7 us -> 6.67 us
  matrix products: 88.5 us -> 95.8 us
    all_to_all x1, waiting for transfers between devices: 30.7 us -> 19.2 us  [forward(): parts = lax.all_to_all(parts, 'space', split_axis=0, concat_axis=0)]
    dot_general x1, matrix products: 13.3 us -> 20.6 us  [forward(): jnp.einsum('ij,bjk->bik', kernel, columns, precision=lax.Precision.HIGHEST)]
    all_to_all x2 -> x0, local copies, waits for them, and re-layouts: 7.27 us -> none  [forward(): lax.all_to_all(along_rows, 'space', split_axis=2, concat_axis=1, tiled=True)]
  transfers between devices with their start and end apart: 10 -> 10, of which waited for: 10 -> 10; matrix products, arithmetic and copies ran while one was open for 4% -> 5% of each run, Pallas kernels for 0% -> 0%
where the time goes in v1:
time: 399 us; the launch traced here: 392 us
  waiting for transfers between devices  218 us (55%)
  matrix products  95.8 us (24%)
  other arithmetic  28.4 us (7%)
  starting transfers between devices  23.1 us (6%)
  blocking collectives  18.6 us (5%)
  local copies, waits for them, and re-layouts  6.67 us (2%)
    ppermute x9, waiting for transfers between devices, shifted(): lax.ppermute(value, axis, [(source, source + steps) for source in range(f...  199 us
    dot_general x1, matrix products, forward(): jnp.einsum('brj,jk->brk', fields, kernel, precision=lax.Precision.HIGHEST)  28.3 us
    dot_general x1, matrix products, inverse(): jnp.einsum('brj,jk->brk', row_layout, kernel, precision=lax.Precision.HIG...  24.2 us
    dot_general x1, matrix products, inverse(): jnp.einsum('ij,bjk->bik', kernel, spectra, precision=lax.Precision.HIGHEST)  22.8 us
    dot_general x1, matrix products, forward(): jnp.einsum('ij,bjk->bik', kernel, columns, precision=lax.Precision.HIGHEST)  20.6 us
    ppermute x9, starting transfers between devices, shifted(): lax.ppermute(value, axis, [(source, source + steps) for source in range(f...  19.4 us
    all_to_all x1, waiting for transfers between devices, forward(): parts = lax.all_to_all(parts, 'space', split_axis=0, concat_axis=0)  19.2 us
    all_to_all x1, blocking collectives, inverse(): lax.all_to_all(along_columns, 'space', split_axis=1, concat_axis=2, tiled...  18.6 us
  transfers between devices with their start and end apart: 10, of which 10 were waited for; matrix products, arithmetic and copies ran while one was open for 5% of the time, Pallas kernels for 0%

profile of v1, /device:TPU:16, one launch (start us, length us, event | category | flops | bytes accessed | tf_op | source)
XLA Modules:
  0.0 391.6 jit_solution(5295262825563427930)
XLA Ops:
  0.0 2.1 fusion.99
  2.1 28.3 %fusion.8 = f32[3,256,1024]{2,1,0:T(8,128)S(1)} fusion(f32[3,256,1024]{2,1,0:T(8,128)S(1)} %fusion.99), kind=kOutput, calls=%fused_computation.11 | convolution fusion | flops 9679405056 | bytes 6291456 | tf_op jit(solution)/shard_map/brj,jk->brk/dot_general | solution.py:42
  30.4 0.3 slice_bitcast_fusion.6
  30.7 2.1 pad_maximum_fusion
  32.7 3.7 all-to-all-start
  36.5 17.7 %fusion.101 = f32[1024,1024,1]{1,0,2:T(8,128)} fusion(), kind=kLoop, calls=%fused_computation.10.clone.clone.clone.1 | loop fusion | flops 15728640 | bytes 4194304 | tf_op jit(solution)/shard_map/ij,bjk->bik/dot_general | solution.py:47
  54.1 19.2 %all-to-all-done = f32[4,3,256,256]{3,2,1,0:T(8,128)S(1)} async-done(((f32[4,3,256,256]{3,2,1,0:T(8,128)}), f32[4,3,256,256]{3,2,1,0:T(8,128)S(1)}, u32[]{:S(2)}, u32[]{:S(2)}) %all-to-all-start) | async-done | bytes 3145760 | tf_op jit(solution)/shard_map/all_to_all | solution.py:45
  73.3 0.0 copy-start
  73.3 0.2 copy.19
  73.5 2.0 copy-done
  75.5 20.6 %fusion.20 = f32[3,1024,256]{1,2,0:T(8,128)S(1)} fusion(f32[3,1024,256]{2,1,0:T(8,128)S(1)} %bitcast.57, f32[1024,1024,1]{1,0,2:T(8,128)S(1)} %copy-done), kind=kOutput, calls=%fused_computation.27 | convolution fusion | flops 9663676416 | bytes 10485760 | tf_op jit(solution)/shard_map/ij,bjk->bik/dot_general | solution.py:47
  96.1 1.0 slice_bitcast_fusion.1
  97.1 3.4 collective-permute-start.1
  100.7 24.2 %collective-permute-done.1 = f32[1024,256]{0,1:T(8,128)} collective-permute-done((f32[1024,256]{0,1:T(8,128)}, f32[1024,256]{0,1:T(8,128)}, u32[]{:S(2)}, u32[]{:S(2)}) %collective-permute-start.1) | collective-permute-done | bytes 1048608 | tf_op jit(solution)/shard_map/ppermute | solution.py:14
  124.8 2.6 multiply_add_fusion.1
  127.4 0.0 copy-start.1
  127.4 2.5 collective-permute-start.2
  130.0 24.0 %collective-permute-done.2 = f32[1024,256]{0,1:T(8,128)S(1)} collective-permute-done((f32[1024,256]{0,1:T(8,128)S(1)}, f32[1024,256]{0,1:T(8,128)S(1)}, u32[]{:S(2)}, u32[]{:S(2)}) %collective-permute-start.2) | collective-permute-done | bytes 1048608 | tf_op jit(solution)/shard_map/ppermute | solution.py:14
  154.0 0.0 copy-done.1
  154.0 2.0 subtract_add_fusion
  156.0 1.6 copy.22
  157.5 0.1 broadcast.36.clone
  157.6 166.7 %while.11 = (s32[]{:T(128)}, f32[1024,256]{1,0:T(8,128)S(1)}, f32[1024,256]{1,0:T(8,128)S(1)}, f32[256]{0:T(256)S(1)}, f32[1024]{0:T(1024)S(1)}, /*index=5*/s32[]{:T(128)}) while((s32[]{:T(128)}, f32[1024,256]{1,0:T(8,128)S(1)}, f32[1024,256]{1,0:T(8,128)S(1)}, f32[256]{0:T(256)S(1)}, f32[1024]{0:T(1024)S(1)}, ...), condition=%wide.region_1.2_spmd.clone, body=%wide.region_0.1_spmd.clone.sunk | while | flops 1572866 | bytes 7345261 | solution.py:77
  158.0 0.3 fusion.104
  158.3 1.9 collective-permute-start
  160.2 23.8 %collective-permute-done = f32[1024,256]{1,0:T(8,128)S(1)} collective-permute-done((f32[1024,256]{1,0:T(8,128)S(1)}, f32[1024,256]{1,0:T(8,128)S(1)}, u32[]{:S(2)}, u32[]{:S(2)}) %collective-permute-start) | collective-permute-done | bytes 1048608 | tf_op jit(solution)/shard_map/while/body/eval_jaxpr/ppermute | solution.py:14
  184.0 0.3 fusion.104
  184.3 1.9 collective-permute-start
  186.2 22.9 %collective-permute-done = f32[1024,256]{1,0:T(8,128)S(1)} collective-permute-done((f32[1024,256]{1,0:T(8,128)S(1)}, f32[1024,256]{1,0:T(8,128)S(1)}, u32[]{:S(2)}, u32[]{:S(2)}) %collective-permute-start) | collective-permute-done | bytes 1048608 | tf_op jit(solution)/shard_map/while/body/eval_jaxpr/ppermute | solution.py:14
  209.1 0.3 fusion.104
  209.4 1.9 collective-permute-start
  211.3 22.0 %collective-permute-done = f32[1024,256]{1,0:T(8,128)S(1)} collective-permute-done((f32[1024,256]{1,0:T(8,128)S(1)}, f32[1024,256]{1,0:T(8,128)S(1)}, u32[]{:S(2)}, u32[]{:S(2)}) %collective-permute-start) | collective-permute-done | bytes 1048608 | tf_op jit(solution)/shard_map/while/body/eval_jaxpr/ppermute | solution.py:14
  233.4 0.3 fusion.104
  233.7 1.9 collective-permute-start
  235.6 21.2 %collective-permute-done = f32[1024,256]{1,0:T(8,128)S(1)} collective-permute-done((f32[1024,256]{1,0:T(8,128)S(1)}, f32[1024,256]{1,0:T(8,128)S(1)}, u32[]{:S(2)}, u32[]{:S(2)}) %collective-permute-start) | collective-permute-done | bytes 1048608 | tf_op jit(solution)/shard_map/while/body/eval_jaxpr/ppermute | solution.py:14
  256.8 0.3 fusion.104
  257.1 1.9 collective-permute-start
  259.0 21.1 %collective-permute-done = f32[1024,256]{1,0:T(8,128)S(1)} collective-permute-done((f32[1024,256]{1,0:T(8,128)S(1)}, f32[1024,256]{1,0:T(8,128)S(1)}, u32[]{:S(2)}, u32[]{:S(2)}) %collective-permute-start) | collective-permute-done | bytes 1048608 | tf_op jit(solution)/shard_map/while/body/eval_jaxpr/ppermute | solution.py:14
  280.1 0.3 fusion.104
  280.4 1.9 collective-permute-start
  282.3 21.1 %collective-permute-done = f32[1024,256]{1,0:T(8,128)S(1)} collective-permute-done((f32[1024,256]{1,0:T(8,128)S(1)}, f32[1024,256]{1,0:T(8,128)S(1)}, u32[]{:S(2)}, u32[]{:S(2)}) %collective-permute-start) | collective-permute-done | bytes 1048608 | tf_op jit(solution)/shard_map/while/body/eval_jaxpr/ppermute | solution.py:14
  303.4 0.3 fusion.104
  303.7 1.9 collective-permute-start
  305.6 18.6 %collective-permute-done = f32[1024,256]{1,0:T(8,128)S(1)} collective-permute-done((f32[1024,256]{1,0:T(8,128)S(1)}, f32[1024,256]{1,0:T(8,128)S(1)}, u32[]{:S(2)}, u32[]{:S(2)}) %collective-permute-start) | collective-permute-done | bytes 1048608 | tf_op jit(solution)/shard_map/while/body/eval_jaxpr/ppermute | solution.py:14
  324.3 0.3 copy.23
  324.6 22.8 %fusion.27 = f32[1,1024,256]{1,2,0:T(8,128)S(1)} fusion(f32[1024,256]{0,1:T(8,128)} %copy-done.1, f32[1024,256]{0,1:T(8,128)} %subtract_add_fusion, f32[1024,256]{0,1:T(8,128)S(1)} %copy.23, f32[256]{0:T(256)S(1)} %get-tuple-element.135, f32[1024]{0:T(1024)S(1)} %get-tuple-element.134), kind=kOutput, calls=%fused_computation.34 | convolution fusion | flops 3238789120 | bytes 4199424 | tf_op jit(solution)/shard_map/ij,bjk->bik/dot_general | solution.py:52
  347.4 0.8 copy.24
  348.2 18.6 %all_to_all.20 = f32[1,1024,256]{2,0,1:T(1,128)S(1)} all-to-all(f32[1,1024,256]{2,0,1:T(1,128)S(1)} %copy.24), channel_id=1, replica_groups=mesh['tm'=8,'space'=4] {'space'}, dimensions={1} | all-to-all | bytes 2097152 | tf_op jit(solution)/shard_map/all_to_all | solution.py:53
  366.8 0.1 copy.27
  366.9 0.3 copy.25
  367.3 24.2 %fusion.29 = f32[1,256,1024]{2,1,0:T(8,128)} fusion(f32[256,1024]{0,1:T(8,128)S(1)} %bitcast.59), kind=kOutput, calls=%fused_computation.36 | convolution fusion | flops 3237216256 | bytes 2097152 | tf_op jit(solution)/shard_map/brj,jk->brk/dot_general | solution.py:54
  (2 shorter events, 0.1 us)
Async XLA Ops:
  32.7 40.6 %all-to-all-start = ((f32[4,3,256,256]{3,2,1,0:T(8,128)}), f32[4,3,256,256]{3,2,1,0:T(8,128)S(1)}, u32[]{:S(2)}, u32[]{:S(2)}) async-start(f32[4,3,256,256]{3,2,1,0:T(8,128)} %pad_maximum_fusion), calls=%async_computation | async-start | bytes 6291456 | tf_op jit(solution)/shard_map/all_to_all | solution.py:45
  73.3 2.2 copy-start
  97.1 27.7 %collective-permute-start.1 = (f32[1024,256]{0,1:T(8,128)}, f32[1024,256]{0,1:T(8,128)}, u32[]{:S(2)}, u32[]{:S(2)}) collective-permute-start(f32[1024,256]{0,1:T(8,128)} %slice_bitcast_fusion.1), channel_id=1, source_target_pairs={{0,4},{4,8},{8,12},{12,16},{16,20},{20,24},{24,28},{1,5},{5,9},{9,... | collective-permute-start | bytes 3145736 | tf_op jit(solution)/shard_map/ppermute | solution.py:14
  127.4 26.6 %copy-start.1 = (f32[1024,256]{0,1:T(8,128)}, f32[1024,256]{0,1:T(8,128)S(1)}, u32[]{:S(2)}) copy-start(f32[1024,256]{0,1:T(8,128)S(1)} %get-tuple-element.72) | copy-start | bytes 3145732
  127.4 26.5 %collective-permute-start.2 = (f32[1024,256]{0,1:T(8,128)S(1)}, f32[1024,256]{0,1:T(8,128)S(1)}, u32[]{:S(2)}, u32[]{:S(2)}) collective-permute-start(f32[1024,256]{0,1:T(8,128)S(1)} %get-tuple-element.72), channel_id=1, source_target_pairs={{0,4},{4,8},{8,12},{12,16},{16,20},{20,24},{24,28},{1,5},{5,9},{9,... | collective-permute-start | bytes 3145736 | tf_op jit(solution)/shard_map/ppermute | solution.py:14
  158.3 25.7 %collective-permute-start = (f32[1024,256]{1,0:T(8,128)S(1)}, f32[1024,256]{1,0:T(8,128)S(1)}, u32[]{:S(2)}, u32[]{:S(2)}) collective-permute-start(f32[1024,256]{1,0:T(8,128)S(1)} %fusion.104), channel_id=1, source_target_pairs={{0,4},{4,8},{8,12},{12,16},{16,20},{20,24},{24,28},{1,5},{5,9},{9,... | collective-permute-start | bytes 3145736 | tf_op jit(solution)/shard_map/while/body/eval_jaxpr/ppermute | solution.py:14
  184.3 24.8 %collective-permute-start = (f32[1024,256]{1,0:T(8,128)S(1)}, f32[1024,256]{1,0:T(8,128)S(1)}, u32[]{:S(2)}, u32[]{:S(2)}) collective-permute-start(f32[1024,256]{1,0:T(8,128)S(1)} %fusion.104), channel_id=1, source_target_pairs={{0,4},{4,8},{8,12},{12,16},{16,20},{20,24},{24,28},{1,5},{5,9},{9,... | collective-permute-start | bytes 3145736 | tf_op jit(solution)/shard_map/while/body/eval_jaxpr/ppermute | solution.py:14
  209.4 24.0 %collective-permute-start = (f32[1024,256]{1,0:T(8,128)S(1)}, f32[1024,256]{1,0:T(8,128)S(1)}, u32[]{:S(2)}, u32[]{:S(2)}) collective-permute-start(f32[1024,256]{1,0:T(8,128)S(1)} %fusion.104), channel_id=1, source_target_pairs={{0,4},{4,8},{8,12},{12,16},{16,20},{20,24},{24,28},{1,5},{5,9},{9,... | collective-permute-start | bytes 3145736 | tf_op jit(solution)/shard_map/while/body/eval_jaxpr/ppermute | solution.py:14
  233.7 23.1 %collective-permute-start = (f32[1024,256]{1,0:T(8,128)S(1)}, f32[1024,256]{1,0:T(8,128)S(1)}, u32[]{:S(2)}, u32[]{:S(2)}) collective-permute-start(f32[1024,256]{1,0:T(8,128)S(1)} %fusion.104), channel_id=1, source_target_pairs={{0,4},{4,8},{8,12},{12,16},{16,20},{20,24},{24,28},{1,5},{5,9},{9,... | collective-permute-start | bytes 3145736 | tf_op jit(solution)/shard_map/while/body/eval_jaxpr/ppermute | solution.py:14
  257.1 23.0 %collective-permute-start = (f32[1024,256]{1,0:T(8,128)S(1)}, f32[1024,256]{1,0:T(8,128)S(1)}, u32[]{:S(2)}, u32[]{:S(2)}) collective-permute-start(f32[1024,256]{1,0:T(8,128)S(1)} %fusion.104), channel_id=1, source_target_pairs={{0,4},{4,8},{8,12},{12,16},{16,20},{20,24},{24,28},{1,5},{5,9},{9,... | collective-permute-start | bytes 3145736 | tf_op jit(solution)/shard_map/while/body/eval_jaxpr/ppermute | solution.py:14
  280.4 23.0 %collective-permute-start = (f32[1024,256]{1,0:T(8,128)S(1)}, f32[1024,256]{1,0:T(8,128)S(1)}, u32[]{:S(2)}, u32[]{:S(2)}) collective-permute-start(f32[1024,256]{1,0:T(8,128)S(1)} %fusion.104), channel_id=1, source_target_pairs={{0,4},{4,8},{8,12},{12,16},{16,20},{20,24},{24,28},{1,5},{5,9},{9,... | collective-permute-start | bytes 3145736 | tf_op jit(solution)/shard_map/while/body/eval_jaxpr/ppermute | solution.py:14
  303.7 20.6 %collective-permute-start = (f32[1024,256]{1,0:T(8,128)S(1)}, f32[1024,256]{1,0:T(8,128)S(1)}, u32[]{:S(2)}, u32[]{:S(2)}) collective-permute-start(f32[1024,256]{1,0:T(8,128)S(1)} %fusion.104), channel_id=1, source_target_pairs={{0,4},{4,8},{8,12},{12,16},{16,20},{20,24},{24,28},{1,5},{5,9},{9,... | collective-permute-start | bytes 3145736 | tf_op jit(solution)/shard_map/while/body/eval_jaxpr/ppermute | solution.py:14
